TPU v7x, 768 devices: a whole 4x8x12 slice. The times are simulated.
768 devices in a mesh: group: 4 (over x), member: 8 (over z_hi, core), space: 24 (over z_lo, y).
Axes of the slice: x: 4, y: 8, z: 12 (z_hi: 4, z_lo: 3; z = z_hi * 3 + z_lo), core: 2. Of those that a mesh axis runs over, the one named last changes fastest.
Arguments:
- height_velocity_tensor: float32 [256, 3, 768, 128], P(('group', 'member'), None, 'space'), may hold values from -6 to 6
- obs_values: float32 [768, 192], P(('group', 'member', 'space')), may hold values from -6 to 6
- obs_precision: float32 [768, 192], P(('group', 'member', 'space')), may hold values from 0.3 to 3
- obs_index: int32 [768, 192], P(('group', 'member', 'space')), may hold values from 0 to 383, as said below
Outputs:
- analysis: float32 [256, 3, 768, 128], P(('group', 'member'), None, 'space')
Inputs may be any that keep to these rules, and one draw needn't show every extreme that they name: `obs_index`: each row holds 192 distinct positions among the 384 values of its block.
All inputs are finite; a program needn't handle non-finite values.
Results may differ from a plain program's by a relative error of at most 0.00013.
Values sent between devices are 32-bit elements; how exact they have to be, the bound alone decides.
A program may use at most 32 MiB of HBM per device.

v0:
```python
import math

import jax
import jax.numpy as jnp
from jax import lax
from jax.sharding import PartitionSpec as P

STEPS = 2


grav_coef = 0.4
depth_coef = 0.4


def padded(cells, sides, width):
    for axis, dim in sides:
        count = lax.axis_size(axis)
        ends = count - 1
        head = lax.slice_in_dim(cells, 0, width, axis=dim)
        tail = lax.slice_in_dim(cells, cells.shape[dim] - width, cells.shape[dim], axis=dim)
        cells = jnp.concatenate(
            [
                lax.ppermute(tail, axis, [(i, (i + 1) % count) for i in range(ends)]),
                cells,
                lax.ppermute(head, axis, [((i + 1) % count, i) for i in range(ends)]),
            ],
            axis=dim,
        )
    return cells


def across_y(field):
    return jnp.roll(field, -1, axis=-1) - jnp.roll(field, 1, axis=-1)


def make_transform(gram, pull):
    identity = jnp.eye(gram.shape[0], dtype=jnp.float32)
    factor = jnp.linalg.cholesky(identity + gram)
    inverse = jax.scipy.linalg.solve_triangular(factor, identity, lower=True)
    inner = jnp.dot(inverse, pull, precision=lax.Precision.HIGHEST)
    weights_mean = jnp.dot(inverse.T, inner, precision=lax.Precision.HIGHEST)
    return inverse + weights_mean[None, :]


def predicted_margins(height_velocity_tensor):
    height, flow_x, flow_y = (
        height_velocity_tensor[:, 0],
        height_velocity_tensor[:, 1],
        height_velocity_tensor[:, 2],
    )
    for stepped in range(STEPS):
        height_ext = padded(height, (("space", 1),), 1)
        new_x = flow_x - grav_coef * (height_ext[:, 2:] - height_ext[:, :-2])
        new_y = flow_y - grav_coef * across_y(height)
        flow_ext = padded(new_x, (("space", 1),), 1)
        height = height - depth_coef * (flow_ext[:, 2:] - flow_ext[:, :-2] + across_y(new_y))
        flow_x, flow_y = (new_x, new_y)
    return jnp.stack([height, flow_x, flow_y], axis=1)


def total_terms(first_term, second_term):
    whole_first, whole_second = lax.psum((first_term, second_term), ("group", "member", "space"))
    return (whole_first, whole_second)


def on_device(height_velocity_tensor, obs_values, obs_precision, obs_index):
    predicted_model_vector = predicted_margins(height_velocity_tensor)
    trajectory_slices, layered_quantities, horizontal_slices, vertical_slices = (
        predicted_model_vector.shape
    )
    trajectory_clusters = lax.axis_size("group") * lax.axis_size("member")
    block_cell_values = horizontal_slices * vertical_slices // trajectory_clusters
    arrived = lax.all_to_all(
        predicted_model_vector, ("group", "member"), split_axis=2, concat_axis=0, tiled=True
    )
    members = arrived.shape[0]
    values = arrived.reshape(members, layered_quantities * block_cell_values)
    ens_mean = jnp.mean(values, axis=0)
    anomaly = values - ens_mean
    positions = obs_index[0]
    precision = obs_precision[0]
    scale = 1.0 / math.sqrt(members - 1)
    seen = jnp.take(anomaly, positions, axis=1)
    seen_mean = jnp.take(ens_mean, positions, axis=0)
    scaled = seen * precision[None, :] * scale
    innovation = precision * (obs_values[0] - seen_mean) * scale
    gram_part = jnp.dot(scaled, scaled.T, precision=lax.Precision.HIGHEST)
    pull_part = jnp.dot(scaled, innovation, precision=lax.Precision.HIGHEST)
    gram, pull = total_terms(gram_part, pull_part)
    transform = make_transform(gram, pull)
    update = jnp.dot(transform, anomaly, precision=lax.Precision.HIGHEST)
    updated = (ens_mean[None, :] + update).reshape(
        members, layered_quantities, 1, block_cell_values
    )
    returned = lax.all_to_all(updated, ("group", "member"), split_axis=0, concat_axis=2, tiled=True)
    return returned


def solution(mesh):
    return jax.shard_map(
        on_device,
        mesh=mesh,
        in_specs=(
            P(("group", "member"), None, "space", None),
            P(("group", "member", "space"), None),
            P(("group", "member", "space"), None),
            P(("group", "member", "space"), None),
        ),
        out_specs=P(("group", "member"), None, "space", None),
        check_vma=False,
    )
```

profile of v0, /device:TPU:1, one launch (start us, length us, event | category | flops | bytes accessed | tf_op | source)
XLA Modules:
  0.0 685.6 jit_solution(2794705721253951079)
XLA Ops:
  9.0 4.8 collective-permute-start.1
  13.8 1.3 collective-permute-start
  16.9 2.5 collective-permute-done.1
  19.4 4.6 collective-permute-done
  24.0 1.7 fusion.14
  25.9 6.9 %collective-permute-start.3 = (f32[8,1,128]{1,0,2:T(8,128)S(1)}, f32[8,1,128]{1,0,2:T(8,128)S(1)}, u32[]{:S(2)}, u32[]{:S(2)}) collective-permute-start(f32[8,1,128]{1,0,2:T(8,128)S(1)} %get-tuple-element.54), channel_id=1, source_target_pairs={{0,1},{1,2},{2,3},{3,4},{4,5},{5,6},{6,7},{7,8},{8,9},{9,10},{10,1... | collective-permute-start | bytes 12296 | tf_op jit(solution)/shard_map/ppermute | solution.py:23
  32.8 1.3 collective-permute-start.2
  34.1 6.6 collective-permute-done.3
  40.7 6.2 collective-permute-done.2
  47.8 4.8 collective-permute-start.5
  52.6 1.3 collective-permute-start.4
  55.3 5.7 collective-permute-done.5
  61.0 3.9 collective-permute-done.4
  65.5 2.9 collective-permute-start.7
  68.5 1.3 collective-permute-start.6
  69.8 5.6 collective-permute-done.7
  75.4 4.3 collective-permute-done.6
  80.3 1.2 copy.182
  81.6 22.3 %all-to-all-start = ((f32[8,3,32,128]{3,0,1,2:T(8,128)}), f32[8,3,32,128]{3,0,1,2:T(8,128)S(1)}, u32[]{:S(2)}, u32[]{:S(2)}) async-start(f32[8,3,32,128]{3,0,1,2:T(8,128)} %copy.182), calls=%async_computation | async-start | bytes 786432 | tf_op jit(solution)/shard_map/all_to_all | solution.py:73
  104.1 15.1 %all-to-all-done = f32[8,3,32,128]{3,0,1,2:T(8,128)S(1)} async-done(((f32[8,3,32,128]{3,0,1,2:T(8,128)}), f32[8,3,32,128]{3,0,1,2:T(8,128)S(1)}, u32[]{:S(2)}, u32[]{:S(2)}) %all-to-all-start) | async-done | bytes 393248 | tf_op jit(solution)/shard_map/all_to_all | solution.py:73
  119.5 1.6 gather_fusion.1
  122.0 1.5 fusion.29
  123.8 114.0 %psum.15 = f32[256]{0:T(256)S(1)} all-reduce(f32[256]{0:T(256)S(1)} %bitcast.110), channel_id=1, replica_groups=mesh['group'=4,'member'=8,'space'=24] {'group','member','space'}, use_global_device_ids=true, to_apply=%region_6.7 | all-reduce | flops 256 | bytes 2048 | tf_op jit(solution)/shard_map/psum | solution.py:62
  237.8 346.0 %all-reduce.3.cloned.1.call-done = f32[256,256]{0,1:T(8,128)} async-done(((f32[256,256]{0,1:T(8,128)}), f32[256,256]{0,1:T(8,128)}) %all-reduce.3.cloned.1.call-update) | async-done | bytes 262160 | tf_op jit(solution)/shard_map/psum | solution.py:62
  585.9 11.7 %cholesky.50 = f32[128,128]{1,0:T(8,128)S(1)} custom-call(f32[128,128]{1,0:T(8,128)S(1)} %cholesky.118), custom_call_target="Cholesky" | custom-call | tf_op jit(solution)/shard_map/jit(cholesky)/cholesky | solution.py:38
  597.7 9.8 %custom-call.15 = f32[1,128,128]{1,2,0:T(8,128)S(1)} custom-call(f32[1,128,128]{2,1,0:T(8,128)S(1)} %get-tuple-element.63), custom_call_target="InvertDiagBlocksLowerTriangular" | custom-call | tf_op jit(solution)/shard_map/jit(cholesky)/cholesky | solution.py:38
  608.0 11.7 %cholesky.105 = f32[128,128]{1,0:T(8,128)S(1)} custom-call(f32[128,128]{1,0:T(8,128)S(1)} %convolution_subtract_fusion.1), custom_call_target="Cholesky" | custom-call | tf_op jit(solution)/shard_map/jit(cholesky)/cholesky | solution.py:38
  621.7 3.8 while.1
  622.3 1.3 bitcast_dynamic-update-slice_fusion.2
  624.2 1.3 bitcast_dynamic-update-slice_fusion.2
  625.5 19.9 %custom-call.16 = f32[2,128,128]{1,2,0:T(8,128)S(1)} custom-call(f32[2,128,128]{2,1,0:T(8,128)S(1)} %get-tuple-element.12), custom_call_target="InvertDiagBlocksLowerTriangular" | custom-call | tf_op jit(solution)/shard_map/jit(_solve_triangular)/triangular_solve | solution.py:39
  648.1 29.8 %all_to_all.33 = f32[256,3,1,128]{3,2,1,0:T(1,128)S(1)} all-to-all(f32[256,3,1,128]{3,2,1,0:T(1,128)S(1)} %copy.188), channel_id=1, replica_groups=mesh['group'=4,'member'=8,'space'=24] {'group','member'}, dimensions={0} | all-to-all | bytes 786432 | tf_op jit(solution)/shard_map/all_to_all | solution.py:95
  (74 shorter events, 17.6 us)
Async XLA Ops:
  9.0 10.5 %collective-permute-start.1 = (f32[8,1,128]{1,0,2:T(8,128)}, f32[8,1,128]{1,0,2:T(8,128)}, u32[]{:S(2)}, u32[]{:S(2)}) collective-permute-start(f32[8,1,128]{1,0,2:T(8,128)} %get-tuple-element.56), channel_id=1, source_target_pairs={{0,1},{1,2},{2,3},{3,4},{4,5},{5,6},{6,7},{7,8},{8,9},{9,10},{10,1... | collective-permute-start | bytes 12296 | tf_op jit(solution)/shard_map/ppermute | solution.py:23
  13.8 10.2 %collective-permute-start = (f32[8,1,128]{1,0,2:T(8,128)}, f32[8,1,128]{1,0,2:T(8,128)}, u32[]{:S(2)}, u32[]{:S(2)}) collective-permute-start(f32[8,1,128]{1,0,2:T(8,128)} %get-tuple-element.55), channel_id=1, source_target_pairs={{1,0},{2,1},{3,2},{4,3},{5,4},{6,5},{7,6},{8,7},{9,8},{10,9},{11,1... | collective-permute-start | bytes 12296 | tf_op jit(solution)/shard_map/ppermute | solution.py:25
  25.9 14.8 %collective-permute-start.3 = (f32[8,1,128]{1,0,2:T(8,128)S(1)}, f32[8,1,128]{1,0,2:T(8,128)S(1)}, u32[]{:S(2)}, u32[]{:S(2)}) collective-permute-start(f32[8,1,128]{1,0,2:T(8,128)S(1)} %get-tuple-element.54), channel_id=1, source_target_pairs={{0,1},{1,2},{2,3},{3,4},{4,5},{5,6},{6,7},{7,8},{8,9},{9,10},{10,1... | collective-permute-start | bytes 12296 | tf_op jit(solution)/shard_map/ppermute | solution.py:23
  32.8 14.1 %collective-permute-start.2 = (f32[8,1,128]{1,0,2:T(8,128)S(1)}, f32[8,1,128]{1,0,2:T(8,128)S(1)}, u32[]{:S(2)}, u32[]{:S(2)}) collective-permute-start(f32[8,1,128]{1,0,2:T(8,128)S(1)} %get-tuple-element.53), channel_id=1, source_target_pairs={{1,0},{2,1},{3,2},{4,3},{5,4},{6,5},{7,6},{8,7},{9,8},{10,9},{11,1... | collective-permute-start | bytes 12296 | tf_op jit(solution)/shard_map/ppermute | solution.py:25
  47.8 13.2 %collective-permute-start.5 = (f32[8,1,128]{1,0,2:T(8,128)S(1)}, f32[8,1,128]{1,0,2:T(8,128)S(1)}, u32[]{:S(2)}, u32[]{:S(2)}) collective-permute-start(f32[8,1,128]{1,0,2:T(8,128)S(1)} %get-tuple-element.40), channel_id=1, source_target_pairs={{0,1},{1,2},{2,3},{3,4},{4,5},{5,6},{6,7},{7,8},{8,9},{9,10},{10,1... | collective-permute-start | bytes 12296 | tf_op jit(solution)/shard_map/ppermute | solution.py:23
  52.6 12.2 %collective-permute-start.4 = (f32[8,1,128]{1,0,2:T(8,128)S(1)}, f32[8,1,128]{1,0,2:T(8,128)S(1)}, u32[]{:S(2)}, u32[]{:S(2)}) collective-permute-start(f32[8,1,128]{1,0,2:T(8,128)S(1)} %get-tuple-element.39), channel_id=1, source_target_pairs={{1,0},{2,1},{3,2},{4,3},{5,4},{6,5},{7,6},{8,7},{9,8},{10,9},{11,1... | collective-permute-start | bytes 12296 | tf_op jit(solution)/shard_map/ppermute | solution.py:25
  53.9 1.0 copy-start
  53.9 1.2 copy-start.1
  65.5 9.9 %collective-permute-start.7 = (f32[8,1,128]{1,0,2:T(8,128)S(1)}, f32[8,1,128]{1,0,2:T(8,128)S(1)}, u32[]{:S(2)}, u32[]{:S(2)}) collective-permute-start(f32[8,1,128]{1,0,2:T(8,128)S(1)} %get-tuple-element.38), channel_id=1, source_target_pairs={{0,1},{1,2},{2,3},{3,4},{4,5},{5,6},{6,7},{7,8},{8,9},{9,10},{10,1... | collective-permute-start | bytes 12296 | tf_op jit(solution)/shard_map/ppermute | solution.py:23
  68.5 11.2 %collective-permute-start.6 = (f32[8,1,128]{1,0,2:T(8,128)S(1)}, f32[8,1,128]{1,0,2:T(8,128)S(1)}, u32[]{:S(2)}, u32[]{:S(2)}) collective-permute-start(f32[8,1,128]{1,0,2:T(8,128)S(1)} %get-tuple-element.37), channel_id=1, source_target_pairs={{1,0},{2,1},{3,2},{4,3},{5,4},{6,5},{7,6},{8,7},{9,8},{10,9},{11,1... | collective-permute-start | bytes 12296 | tf_op jit(solution)/shard_map/ppermute | solution.py:25
  80.3 23.7 %copy-start.3 = (s32[1,192]{1,0:T(1,128)S(1)}, s32[1,192]{1,0:T(1,128)}, u32[]{:S(2)}) copy-start(s32[1,192]{1,0:T(1,128)} %param.7) | copy-start | bytes 2308
  81.6 37.6 %all-to-all-start = ((f32[8,3,32,128]{3,0,1,2:T(8,128)}), f32[8,3,32,128]{3,0,1,2:T(8,128)S(1)}, u32[]{:S(2)}, u32[]{:S(2)}) async-start(f32[8,3,32,128]{3,0,1,2:T(8,128)} %copy.182), calls=%async_computation | async-start | bytes 786432 | tf_op jit(solution)/shard_map/all_to_all | solution.py:73
  103.9 479.9 %all-reduce.3.cloned.1.call-start = ((), (), s32[]{:S(2)}) async-start(), calls=%async_computation.2 | async-start | bytes 524288 | tf_op jit(solution)/shard_map/psum | solution.py:62
  119.4 2.5 copy-start.2
  119.4 2.5 copy-start.4
Sparse Core Ops, SparseCore 0:
  123.6 460.1 all-reduce.2
where the time goes:
time: 687 us; the launch traced here: 686 us
  waiting for transfers between devices  401 us (58%)
  blocking collectives  144 us (21%)
  other arithmetic  59.8 us (9%)
  starting transfers between devices  46.9 us (7%)
  local copies, waits for them, and re-layouts  15.1 us (2%)
  between operations  15.1 us (2%)
    psum x1, waiting for transfers between devices, total_terms(): lax.psum((first_term, second_term), ('group', 'member', 'space'))  346 us
    psum x1, blocking collectives, total_terms(): lax.psum((first_term, second_term), ('group', 'member', 'space'))  114 us
    another operation x6, other arithmetic, make_transform(): factor = jnp.linalg.cholesky(identity + gram)  33.9 us
    all_to_all x1, blocking collectives, on_device(): lax.all_to_all(updated, ('group', 'member'), split_axis=0, concat_axis=2,...  29.8 us
    all_to_all x1, starting transfers between devices, on_device(): lax.all_to_all(predicted_model_vector, ('group', 'member'), split_axis=2,...  22.3 us
    ppermute x4, waiting for transfers between devices, padded(): lax.ppermute(tail, axis, [(i, (i + 1) % count) for i in range(ends)])  20.4 us
    another operation x3, other arithmetic, make_transform(): inverse = jax.scipy.linalg.solve_triangular(factor, identity, lower=True)  19.9 us
    ppermute x4, starting transfers between devices, padded(): lax.ppermute(tail, axis, [(i, (i + 1) % count) for i in range(ends)])  19.4 us
  transfers between devices with their start and end apart: 10, of which 10 were waited for; matrix products, arithmetic and copies ran while one was open for 0% of the time, Pallas kernels for 0%

commit v1 on v0

v1 whole, which is shorter than its diff:
```python
import math

import jax
import jax.numpy as jnp
from jax import lax
from jax.experimental import pallas as pl
from jax.experimental.pallas import tpu as pltpu
from jax.sharding import PartitionSpec as P

GRAV = 0.4
DEPTH = 0.4
GROUPS, MEMBERS, SPACES = 4, 8, 24
NZ, NY_CHIPS = 12, 8
OWNERS = GROUPS * MEMBERS
ROWS = 32
LOCAL = 8
ENSEMBLE = OWNERS * LOCAL
FIELDS = 3
COLS = 128
CELLS = FIELDS * COLS
OBS = 192
HALO = 4
MESH = pl.DeviceIdType.MESH
F32 = jnp.float32
HIGHEST = lax.Precision.HIGHEST
SCALE = 1.0 / math.sqrt(ENSEMBLE - 1)


def dot_nt(a, b):
    return lax.dot_general(
        a, b, (((1,), (1,)), ((), ())), precision=HIGHEST, preferred_element_type=F32
    )


def dot_nn(a, b):
    return lax.dot_general(
        a, b, (((1,), (0,)), ((), ())), precision=HIGHEST, preferred_element_type=F32
    )


def place():
    group = lax.axis_index("group")
    member = lax.axis_index("member")
    space = lax.axis_index("space")
    return group, member, space


def owner_id(k):
    return {"group": k // MEMBERS, "member": lax.rem(k, MEMBERS)}


def z_id(z, core, y):
    return {"member": z // 3 * 2 + core, "space": lax.rem(z, 3) * NY_CHIPS + y}


def across_y(field):
    return pltpu.roll(field, COLS - 1, 1) - pltpu.roll(field, 1, 1)


class Forecast:
    def __init__(self, load, outside):
        self.load = load
        self.outside = outside
        self.known = {}

    def masked(self, row, value):
        flag = self.outside(row)
        return value if flag is None else jnp.where(flag, 0.0, value)

    def get(self, field, step, row):
        key = (field, step, row)
        if key not in self.known:
            self.known[key] = self.compute(field, step, row)
        return self.known[key]

    def compute(self, field, step, row):
        if step == 0:
            return self.masked(row, self.load(field, row))
        if field == 1:
            ahead, behind = self.get(0, step - 1, row + 1), self.get(0, step - 1, row - 1)
            return self.masked(row, self.get(1, step - 1, row) - GRAV * (ahead - behind))
        if field == 2:
            return self.get(2, step - 1, row) - GRAV * across_y(self.get(0, step - 1, row))
        ahead, behind = self.get(1, step, row + 1), self.get(1, step, row - 1)
        change = ahead - behind + across_y(self.get(2, step, row))
        return self.masked(row, self.get(0, step - 1, row) - DEPTH * change)


def gather_kernel(
    x_ref,
    x_halo_ref,
    obs_ref,
    index_ref,
    values_ref,
    gram_ref,
    halo,
    sendbuf,
    mine,
    corebuf,
    x_from,
    x_to,
    y_from,
    y_to,
    z_from,
    z_own,
    all_y,
    all_x,
    halo_send,
    halo_recv,
    a2a_send,
    a2a_recv,
    core_sem,
    x_sem,
    y_sem,
    z_sem,
    gy_sem,
    gx_sem,
    gc_sem,
):
    group, member, space = place()
    core = lax.rem(member, 2)
    z = member // 2 * 3 + space // NY_CHIPS
    y = lax.rem(space, NY_CHIPS)
    me = group * MEMBERS + member

    barrier = pltpu.get_barrier_semaphore()
    above, below = lax.rem(space + SPACES - 1, SPACES), lax.rem(space + 1, SPACES)
    peers = [{"space": above}, {"space": below}]
    peers += [owner_id(lax.rem(me + d, OWNERS)) for d in range(1, OWNERS)]
    y_peers = [
        {"space": space - y + lax.rem(y + d, NY_CHIPS)} for d in range(1, NY_CHIPS)
    ]
    z_peers = [z_id(lax.rem(z + d, NZ), core, y) for d in range(1, NZ)]
    peers += y_peers + z_peers
    for peer in peers:
        pl.semaphore_signal(barrier, inc=1, device_id=peer, device_id_type=MESH)

    cells = lax.broadcasted_iota(jnp.int32, (CELLS, OBS), 0)
    picked = jnp.where(cells == index_ref[0:1, :], 1.0, 0.0)
    spread = dot_nt(obs_ref[...], picked)
    weight = spread[1:2, :] * SCALE
    seen_value = spread[0:1, :]

    pl.semaphore_wait(barrier, len(peers))

    up = pltpu.make_async_remote_copy(
        src_ref=x_halo_ref.at[:, 0],
        dst_ref=halo.at[1],
        send_sem=halo_send.at[0],
        recv_sem=halo_recv.at[1],
        device_id={"space": above},
        device_id_type=MESH,
    )
    down = pltpu.make_async_remote_copy(
        src_ref=x_halo_ref.at[:, ROWS // HALO - 1],
        dst_ref=halo.at[0],
        send_sem=halo_send.at[1],
        recv_sem=halo_recv.at[0],
        device_id={"space": below},
        device_id_type=MESH,
    )
    up.start()
    down.start()

    flat = [halo.at[i].reshape(LOCAL * FIELDS * HALO, COLS) for i in range(2)]

    def load(field, row):
        if row < 0:
            start = field * HALO + row + HALO
            return flat[0][pl.ds(start, LOCAL, stride=FIELDS * HALO), :]
        if row >= ROWS:
            start = field * HALO + row - ROWS
            return flat[1][pl.ds(start, LOCAL, stride=FIELDS * HALO), :]
        return x_ref[pl.ds(field * ROWS + row, LOCAL, stride=FIELDS * ROWS), :]

    first, last = space == 0, space == SPACES - 1

    def outside(row):
        return first if row < 0 else last if row >= ROWS else None

    forecast = Forecast(load, outside)

    def block_copy(k):
        return pltpu.make_async_remote_copy(
            src_ref=sendbuf.at[k],
            dst_ref=values_ref.at[me],
            send_sem=a2a_send.at[k],
            recv_sem=a2a_recv.at[me],
            device_id=owner_id(k),
            device_id_type=MESH,
        )

    def emit(rows):
        for row in rows:
            for field in range(FIELDS):
                sendbuf[row, :, field * COLS : (field + 1) * COLS] = forecast.get(
                    field, STEPS, row
                )

    def start(k):
        @pl.when(k != me)
        def _():
            block_copy(k).start()

    inner = ROWS - 2 * HALO
    emit(range(HALO, ROWS - HALO))
    for d in range(inner):
        start(HALO + lax.rem(me + d, inner))
    up.wait()
    down.wait()
    emit(list(range(HALO)) + list(range(ROWS - HALO, ROWS)))
    for d in range(2 * HALO):
        start(lax.rem(ROWS - HALO + lax.rem(me + d, 2 * HALO), ROWS))
    values_ref[me] = sendbuf[me]
    for d in range(1, OWNERS):
        block_copy(lax.rem(me + d, OWNERS)).wait_send()
    for d in range(1, OWNERS):
        k = lax.rem(me + d, OWNERS)
        pltpu.make_async_remote_copy(
            src_ref=sendbuf.at[k],
            dst_ref=values_ref.at[k],
            send_sem=a2a_send.at[k],
            recv_sem=a2a_recv.at[k],
            device_id=owner_id(k),
            device_id_type=MESH,
        ).wait_recv()

    values = values_ref[...].reshape(ENSEMBLE, CELLS)
    mean = jnp.sum(values, axis=0, keepdims=True) * (1.0 / ENSEMBLE)
    scaled = (values - mean) * weight
    innovation = weight * (seen_value - mean)
    gram = dot_nt(scaled, scaled)
    pull = dot_nt(jnp.broadcast_to(innovation, (8, CELLS)), scaled)[0:1, :]
    left, right = gram[:, :COLS], gram[:, COLS:]
    mine[0] = left
    mine[1] = right
    mine[1, 0:1, :] = pull[:, :COLS]
    mine[1, 1:2, :] = pull[:, COLS:]

    def exchange(src, dst, sem_pair, slot_send, slot_recv, device):
        copy = pltpu.make_async_remote_copy(
            src_ref=src,
            dst_ref=dst,
            send_sem=sem_pair.at[0, slot_send],
            recv_sem=sem_pair.at[1, slot_recv],
            device_id=device,
            device_id_type=MESH,
        )
        copy.start()
        return copy

    partner = {"member": member + 1 - 2 * core}
    copy = exchange(mine.at[1 - core], corebuf, core_sem, 0, 0, partner)
    copy.wait()
    half = mine[core] + corebuf[...]
    x_to[...] = half.reshape(GROUPS, ENSEMBLE // GROUPS, COLS)

    copies = []
    for d in range(1, GROUPS):
        there = lax.rem(group + d, GROUPS)
        copies.append(
            exchange(x_to.at[there], x_from.at[d - 1], x_sem, d - 1, d - 1, {"group": there})
        )
    for copy in copies:
        copy.wait()
    quarter = x_to[group] + (x_from[0] + x_from[1] + x_from[2])
    y_to[...] = quarter.reshape(NY_CHIPS, 8, COLS)

    copies = []
    for d in range(1, NY_CHIPS):
        there = lax.rem(y + d, NY_CHIPS)
        copies.append(
            exchange(y_to.at[there], y_from.at[d - 1], y_sem, d - 1, d - 1, y_peers[d - 1])
        )
    for copy in copies:
        copy.wait()
    tile = y_to[y]
    for d in range(1, NY_CHIPS):
        tile = tile + y_from[d - 1]

    z_own[...] = tile
    z_from[z] = tile
    copies = []
    for d in range(1, NZ):
        copies.append(exchange(z_own, z_from.at[z], z_sem, d - 1, d - 1, z_peers[d - 1]))
    for copy in copies:
        copy.wait()
    total = z_from[0]
    for at in range(1, NZ):
        total = total + z_from[at]

    all_y[y] = total
    copies = []
    for d in range(1, NY_CHIPS):
        copies.append(
            exchange(all_y.at[y], all_y.at[y], gy_sem, d - 1, d - 1, y_peers[d - 1])
        )
    for copy in copies:
        copy.wait()

    x_slice = all_y[...].reshape(ENSEMBLE // GROUPS, COLS)
    all_x[group] = x_slice
    copies = []
    for d in range(1, GROUPS):
        there = lax.rem(group + d, GROUPS)
        copies.append(
            exchange(all_x.at[group], all_x.at[group], gx_sem, d - 1, d - 1, {"group": there})
        )
    for copy in copies:
        copy.wait()

    gram_ref[core] = all_x[...].reshape(ENSEMBLE, COLS)
    copy = exchange(gram_ref.at[core], gram_ref.at[core], gc_sem, 0, 0, partner)
    copy.wait()


STEPS = 2


def gather(state, obs, index):
    vmem = pl.BlockSpec(memory_space=pltpu.VMEM)
    dma = pltpu.SemaphoreType.DMA
    quarter = ENSEMBLE // GROUPS
    return pl.pallas_call(
        gather_kernel,
        out_shape=(
            jax.ShapeDtypeStruct((OWNERS, LOCAL, CELLS), F32),
            jax.ShapeDtypeStruct((2, ENSEMBLE, COLS), F32),
        ),
        in_specs=[vmem, pl.BlockSpec(memory_space=pl.ANY), vmem, vmem],
        out_specs=(vmem, vmem),
        scratch_shapes=[
            pltpu.VMEM((2, LOCAL * FIELDS, HALO, COLS), F32),
            pltpu.VMEM((OWNERS, LOCAL, CELLS), F32),
            pltpu.VMEM((2, ENSEMBLE, COLS), F32),
            pltpu.VMEM((ENSEMBLE, COLS), F32),
            pltpu.VMEM((GROUPS - 1, quarter, COLS), F32),
            pltpu.VMEM((GROUPS, quarter, COLS), F32),
            pltpu.VMEM((NY_CHIPS - 1, 8, COLS), F32),
            pltpu.VMEM((NY_CHIPS, 8, COLS), F32),
            pltpu.VMEM((NZ, 8, COLS), F32),
            pltpu.VMEM((8, COLS), F32),
            pltpu.VMEM((NY_CHIPS, 8, COLS), F32),
            pltpu.VMEM((GROUPS, quarter, COLS), F32),
            dma((2,)),
            dma((2,)),
            dma((OWNERS,)),
            dma((OWNERS,)),
            dma((2, 1)),
            dma((2, GROUPS - 1)),
            dma((2, NY_CHIPS - 1)),
            dma((2, NZ - 1)),
            dma((2, NY_CHIPS - 1)),
            dma((2, GROUPS - 1)),
            dma((2, 1)),
        ],
        compiler_params=pltpu.CompilerParams(collective_id=0, has_side_effects=True),
        name="gather_and_gram",
    )(
        state.reshape(LOCAL * FIELDS * ROWS, COLS),
        state.reshape(LOCAL * FIELDS, ROWS // HALO, HALO, COLS),
        obs,
        index,
    )


def return_kernel(values_ref, transform_ref, out_ref, sendbuf, arrived, send_sem, recv_sem):
    group, member, _ = place()
    me = group * MEMBERS + member
    barrier = pltpu.get_barrier_semaphore()
    for d in range(1, OWNERS):
        pl.semaphore_signal(
            barrier, inc=1, device_id=owner_id(lax.rem(me + d, OWNERS)), device_id_type=MESH
        )
    values = values_ref[...].reshape(ENSEMBLE, CELLS)
    mean = jnp.sum(values, axis=0, keepdims=True) * (1.0 / ENSEMBLE)
    updated = dot_nn(transform_ref[...], values - mean) + mean
    sendbuf[...] = updated.reshape(OWNERS, LOCAL, CELLS)
    pl.semaphore_wait(barrier, OWNERS - 1)

    def copy(k, slot):
        return pltpu.make_async_remote_copy(
            src_ref=sendbuf.at[k],
            dst_ref=arrived.at[slot],
            send_sem=send_sem.at[k],
            recv_sem=recv_sem.at[slot],
            device_id=owner_id(k),
            device_id_type=MESH,
        )

    for d in range(1, OWNERS):
        copy(lax.rem(me + d, OWNERS), me).start()
    arrived[me] = sendbuf[me]
    for d in range(1, OWNERS):
        copy(lax.rem(me + d, OWNERS), me).wait_send()
    for d in range(1, OWNERS):
        k = lax.rem(me + d, OWNERS)
        copy(k, k).wait_recv()
    for row in range(ROWS):
        for field in range(FIELDS):
            out_ref[pl.ds(field * ROWS + row, LOCAL, stride=FIELDS * ROWS), :] = arrived[
                row, :, field * COLS : (field + 1) * COLS
            ]


def give_back(values, transform):
    vmem = pl.BlockSpec(memory_space=pltpu.VMEM)
    dma = pltpu.SemaphoreType.DMA
    out = pl.pallas_call(
        return_kernel,
        out_shape=jax.ShapeDtypeStruct((LOCAL * FIELDS * ROWS, COLS), F32),
        in_specs=[vmem, vmem],
        out_specs=vmem,
        scratch_shapes=[
            pltpu.VMEM((OWNERS, LOCAL, CELLS), F32),
            pltpu.VMEM((OWNERS, LOCAL, CELLS), F32),
            dma((OWNERS,)),
            dma((OWNERS,)),
        ],
        compiler_params=pltpu.CompilerParams(collective_id=1, has_side_effects=True),
        name="update_and_return",
    )(values, transform)
    return out.reshape(LOCAL, FIELDS, ROWS, COLS)


def make_transform(both):
    pull = jnp.concatenate([both[1, 0], both[1, 1]])
    corner = jnp.zeros((COLS, COLS), F32)
    upper = jnp.concatenate([both[0, :COLS], corner], axis=1)
    lower = jnp.concatenate([both[0, COLS:], both[1, COLS:]], axis=1)
    gram = jnp.concatenate([upper, lower], axis=0)
    identity = jnp.eye(ENSEMBLE, dtype=F32)
    factor = lax.linalg.cholesky(identity + gram, symmetrize_input=False)
    inverse = jax.scipy.linalg.solve_triangular(factor, identity, lower=True)
    inner = jnp.dot(inverse, pull, precision=HIGHEST)
    weights_mean = jnp.dot(inverse.T, inner, precision=HIGHEST)
    return inverse + weights_mean[None, :]


def on_device(height_velocity_tensor, obs_values, obs_precision, obs_index):
    obs = jnp.concatenate([obs_values, obs_precision, jnp.zeros((6, OBS), F32)], axis=0)
    values, both = gather(height_velocity_tensor, obs, obs_index)
    return give_back(values, make_transform(both))


def solution(mesh):
    return jax.shard_map(
        on_device,
        mesh=mesh,
        in_specs=(
            P(("group", "member"), None, "space", None),
            P(("group", "member", "space"), None),
            P(("group", "member", "space"), None),
            P(("group", "member", "space"), None),
        ),
        out_specs=P(("group", "member"), None, "space", None),
        check_vma=False,
    )
```

time: 687 us -> 161 us (0.23)
  waiting for transfers between devices: 401 us -> 0 us
  blocking collectives: 144 us -> 0 us
  Pallas kernels: 0 us -> 94.3 us
  starting transfers between devices: 46.9 us -> 0 us
  between operations: 15.1 us -> 1.42 us
  local copies, waits for them, and re-layouts: 15.1 us -> 8.1 us
    psum x1 -> x0, waiting for transfers between devices: 346 us -> none  [total_terms(): lax.psum((first_term, second_term), ('group', 'member', 'space'))]
    psum x1 -> x0, blocking collectives: 114 us -> none  [total_terms(): lax.psum((first_term, second_term), ('group', 'member', 'space'))]
    pallas_call x0 -> x2, Pallas kernels: none -> 94.3 us  [the longest x1 69 us: gather(): pl.pallas_call(gather_kernel, out_shape=(jax.ShapeDtypeStruct((OWNERS, LO...]
    ppermute x8 -> x0, waiting for transfers between devices: 39.4 us -> none  [the longest x4 20.4 us: padded(): lax.ppermute(tail, axis, [(i, (i + 1) % count) for i in range(ends)])]
    all_to_all x1 -> x0, blocking collectives: 29.8 us -> none  [on_device(): lax.all_to_all(updated, ('group', 'member'), split_axis=0, concat_axis=2,...]
    ppermute x8 -> x0, starting transfers between devices: 24.5 us -> none  [the longest x4 19.4 us: padded(): lax.ppermute(tail, axis, [(i, (i + 1) % count) for i in range(ends)])]
    all_to_all x1 -> x0, starting transfers between devices: 22.3 us -> none  [on_device(): lax.all_to_all(predicted_model_vector, ('group', 'member'), split_axis=2,...]
    all_to_all x1 -> x0, waiting for transfers between devices: 15.1 us -> none  [on_device(): lax.all_to_all(predicted_model_vector, ('group', 'member'), split_axis=2,...]
  transfers between devices with their start and end apart: 10 -> 0, of which waited for: 10 -> 0; matrix products, arithmetic and copies ran while one was open for 0% -> 0% of each run, Pallas kernels for 0% -> 0%
where the time goes in v1:
time: 161 us
  Pallas kernels  94.3 us (59%)
  other arithmetic  55.3 us (34%)
  local copies, waits for them, and re-layouts  8.1 us (5%)
  matrix products  1.85 us (1%)
    pallas_call x1, Pallas kernels, gather(): pl.pallas_call(gather_kernel, out_shape=(jax.ShapeDtypeStruct((OWNERS, LO...  69 us
    another operation x6, other arithmetic, make_transform(): factor = lax.linalg.cholesky(identity + gram, symmetrize_input=False)  34.1 us
    pallas_call x1, Pallas kernels, give_back(): pl.pallas_call(return_kernel, out_shape=jax.ShapeDtypeStruct((LOCAL * FIE...  25.4 us
    another operation x3, other arithmetic, make_transform(): inverse = jax.scipy.linalg.solve_triangular(factor, identity, lower=True)  19.7 us
    another operation x6, local copies, waits for them, and re-layouts  3.87 us

profile of v1, /device:TPU:1, one launch (start us, length us, event | category | flops | bytes accessed | tf_op | source)
XLA Modules:
  0.0 161.1 jit_solution(17967934657577174075)
XLA Ops:
  0.0 0.0 copy-start.1
  0.0 0.0 copy-start
  0.0 0.1 pad.13.clone
  0.1 0.6 copy-done.1
  0.7 0.0 copy-done
  0.7 0.7 maximum_maximum_fusion.obs_ref
  1.4 69.0 %gather_and_gram.1 = (f32[32,8,384]{2,1,0:T(8,128)}, f32[2,256,128]{2,1,0:T(8,128)}) custom-call(f32[768,128]{1,0:T(8,128)} %bitcast.50, f32[24,8,4,128]{3,2,1,0:T(4,128)} %bitcast.51, f32[8,192]{1,0:T(8,128)} %maximum_maximum_fusion.obs_ref, s32[1,192]{1,0:T(1,128)} %index_ref.1), custom_call_target="tpu_custom_call" | custom-call | tf_op jit(solution)/shard_map/gather_and_gram/pallas_call | solution.py:324
  70.4 0.9 slice_bitcast_fusion.5
  71.3 11.7 %cholesky.49 = f32[128,128]{1,0:T(8,128)S(1)} custom-call(f32[128,128]{1,0:T(8,128)S(1)} %cholesky.115), custom_call_target="Cholesky" | custom-call | tf_op jit(solution)/shard_map/cholesky | solution.py:433
  83.1 9.8 %custom-call.12 = f32[1,128,128]{1,2,0:T(8,128)S(1)} custom-call(f32[1,128,128]{2,1,0:T(8,128)S(1)} %get-tuple-element.35), custom_call_target="InvertDiagBlocksLowerTriangular" | custom-call | tf_op jit(solution)/shard_map/cholesky | solution.py:433
  92.9 0.2 constant_dynamic-update-slice_fusion.1
  93.1 0.3 convolution_subtract_fusion.1
  93.4 11.9 %cholesky.102 = f32[128,128]{1,0:T(8,128)S(1)} custom-call(f32[128,128]{1,0:T(8,128)S(1)} %convolution_subtract_fusion.1), custom_call_target="Cholesky" | custom-call | tf_op jit(solution)/shard_map/cholesky | solution.py:433
  105.3 0.7 compare_reduce_fusion
  107.3 0.1 triangular_solve.64
  107.4 3.9 %while.1 = (s32[]{:T(128)}, f32[256,256]{1,0:T(8,128)S(1)}, s32[2,2]{1,0:T(2,128)S(1)}, f32[2,128,128]{2,1,0:T(8,128)S(1)}, s32[]{:T(128)}) while((s32[]{:T(128)}, f32[256,256]{1,0:T(8,128)S(1)}, s32[2,2]{1,0:T(2,128)S(1)}, f32[2,128,128]{2,1,0:T(8,128)S(1)}, s32[]{:T(128)}) %tuple.26), condition=%wide.while_cond, body=%wide.while_body.sunk | while | flops 2 | bytes 131181 | solution.py:434
  107.4 0.6 fusion.22
  108.0 1.3 bitcast_dynamic-update-slice_fusion.2
  109.3 0.6 fusion.22
  109.9 1.3 bitcast_dynamic-update-slice_fusion.2
  111.3 19.7 %custom-call.13 = f32[2,128,128]{1,2,0:T(8,128)S(1)} custom-call(f32[2,128,128]{2,1,0:T(8,128)S(1)} %get-tuple-element.16), custom_call_target="InvertDiagBlocksLowerTriangular" | custom-call | tf_op jit(solution)/shard_map/jit(_solve_triangular)/triangular_solve | solution.py:434
  131.0 0.3 fusion.4
  131.3 0.3 convolution_subtract_fusion
  131.6 0.3 fusion.8
  131.9 0.8 slice_bitcast_fusion.8
  132.7 0.3 convolution_bitcast_fusion
  132.9 0.3 fusion.1
  133.2 0.8 fusion.3.transform_ref
  134.0 25.4 %update_and_return.1 = f32[768,128]{1,0:T(8,128)} custom-call(f32[32,8,384]{2,1,0:T(8,128)} %get-tuple-element.7.values_ref, f32[256,256]{1,0:T(8,128)} %fusion.3.transform_ref), custom_call_target="tpu_custom_call" | custom-call | tf_op jit(solution)/shard_map/update_and_return/pallas_call | solution.py:409
  159.3 1.8 %copy.18 = f32[8,3,32,128]{3,2,1,0:T(8,128)} copy(f32[8,3,32,128]{3,2,1,0:T(8,128)} %bitcast.52) | data formatting | bytes 786432
  (14 shorter events, 0.2 us)
Async XLA Ops:
  0.0 0.7 copy-start.1
  0.0 0.7 copy-start

commit v2 on v1

--- a/solution.py
+++ b/solution.py
@@ -20,6 +20,7 @@
 CELLS = FIELDS * COLS
 OBS = 192
 HALO = 4
+BLOCK, SUB = 64, 8
 MESH = pl.DeviceIdType.MESH
 F32 = jnp.float32
 HIGHEST = lax.Precision.HIGHEST
@@ -423,18 +424,113 @@
     return out.reshape(LOCAL, FIELDS, ROWS, COLS)
 
 
+def lane(tile, at):
+    return jnp.broadcast_to(tile[:, at : at + 1], (SUB, COLS))
+
+def sublane(tile, at):
+    return jnp.broadcast_to(tile[at : at + 1, :], (SUB, COLS))
+
+def total(terms):
+    while len(terms) > 1:
+        terms = [a + b for a, b in zip(terms[::2], terms[1::2])] + (
+            [terms[-1]] if len(terms) % 2 else []
+        )
+    return terms[0]
+
+def small_factor(tile, at):
+    columns = [lane(tile, at + j) for j in range(SUB)]
+    left = {(i, j): sublane(columns[j], i) for j in range(SUB) for i in range(j, SUB)}
+    low, inv = {}, {}
+    for j in range(SUB):
+        root = lax.rsqrt(left[j, j])
+        inv[j, j] = root
+        for i in range(j + 1, SUB):
+            low[i, j] = left[i, j] * root
+        for k in range(j + 1, SUB):
+            for i in range(k, SUB):
+                left[i, k] = left[i, k] - low[i, j] * low[k, j]
+    for j in range(SUB):
+        for i in range(j + 1, SUB):
+            terms = [low[i, k] * inv[k, j] for k in range(j, i)]
+            inv[i, j] = -(total(terms) * inv[i, i])
+    return inv
+
+def invert_block(block, identity):
+    wide = jnp.concatenate([block, identity], axis=1)
+    tiles = [wide[SUB * q : SUB * (q + 1)] for q in range(BLOCK // SUB)]
+    rows = lax.broadcasted_iota(jnp.int32, (SUB, COLS), 0)
+    count = len(tiles)
+    for p in range(count):
+        inv = small_factor(tiles[p], SUB * p)
+        terms = []
+        for j in range(SUB):
+            column = inv[SUB - 1, j]
+            for i in range(SUB - 2, j - 1, -1):
+                column = jnp.where(rows <= i, inv[i, j], column)
+            if j > 0:
+                column = jnp.where(rows < j, 0.0, column)
+            terms.append(column * sublane(tiles[p], j))
+        done = total(terms)
+        spread = [sublane(done, k) for k in range(SUB)]
+        for q in range(p + 1, count):
+            source = [lane(tiles[q], SUB * p + j) for j in range(SUB)]
+            terms = [
+                total([inv[k, j] * source[j] for j in range(k + 1)]) * spread[k]
+                for k in range(SUB)
+            ]
+            tiles[q] = tiles[q] - total(terms)
+        tiles[p] = done
+    return jnp.concatenate(tiles, axis=0)[:, BLOCK:]
+
+def invert(work):
+    n = ENSEMBLE // BLOCK
+    r = lax.broadcasted_iota(jnp.int32, (BLOCK, BLOCK), 0)
+    c = lax.broadcasted_iota(jnp.int32, (BLOCK, BLOCK), 1)
+    identity = jnp.where(r == c, 1.0, 0.0)
+    zero = jnp.zeros((BLOCK, BLOCK), F32)
+    for k in range(n):
+        at = k * BLOCK
+        own = slice(at, at + BLOCK)
+        rest = slice(at + BLOCK, ENSEMBLE)
+        inverse = invert_block(work[own, own], identity)
+        if k < n - 1:
+            factor = dot_nt(work[rest, own], inverse)
+        work[own, own] = identity
+        solved = dot_nn(inverse, work[own, :])
+        work[own, :] = solved
+        if k < n - 1:
+            work[rest, own] = jnp.zeros((ENSEMBLE - at - BLOCK, BLOCK), F32)
+            work[rest, :] = work[rest, :] - dot_nn(factor, solved)
+
+def transform_kernel(both_ref, transform_ref, work):
+    r = lax.broadcasted_iota(jnp.int32, (COLS, COLS), 0)
+    c = lax.broadcasted_iota(jnp.int32, (COLS, COLS), 1)
+    eye = jnp.where(r == c, 1.0, 0.0)
+    below = both_ref[0, COLS:, :]
+    work[:COLS, :COLS] = both_ref[0, :COLS, :] + eye
+    work[COLS:, :COLS] = below
+    work[:COLS, COLS:] = below.T
+    work[COLS:, COLS:] = both_ref[1, COLS:, :] + eye
+    pull = jnp.concatenate([both_ref[1, 0:1, :], both_ref[1, 1:2, :]], axis=1)
+    invert(work)
+    r = lax.broadcasted_iota(jnp.int32, (ENSEMBLE, ENSEMBLE), 0)
+    c = lax.broadcasted_iota(jnp.int32, (ENSEMBLE, ENSEMBLE), 1)
+    inverse = jnp.where(r >= c, work[...], 0.0)
+    inner = dot_nt(jnp.broadcast_to(pull, (SUB, ENSEMBLE)), inverse)
+    weights = dot_nn(inner, inverse)
+    transform_ref[...] = inverse + weights[0:1, :]
+
+
 def make_transform(both):
-    pull = jnp.concatenate([both[1, 0], both[1, 1]])
-    corner = jnp.zeros((COLS, COLS), F32)
-    upper = jnp.concatenate([both[0, :COLS], corner], axis=1)
-    lower = jnp.concatenate([both[0, COLS:], both[1, COLS:]], axis=1)
-    gram = jnp.concatenate([upper, lower], axis=0)
-    identity = jnp.eye(ENSEMBLE, dtype=F32)
-    factor = lax.linalg.cholesky(identity + gram, symmetrize_input=False)
-    inverse = jax.scipy.linalg.solve_triangular(factor, identity, lower=True)
-    inner = jnp.dot(inverse, pull, precision=HIGHEST)
-    weights_mean = jnp.dot(inverse.T, inner, precision=HIGHEST)
-    return inverse + weights_mean[None, :]
+    vmem = pl.BlockSpec(memory_space=pltpu.VMEM)
+    return pl.pallas_call(
+        transform_kernel,
+        out_shape=jax.ShapeDtypeStruct((ENSEMBLE, ENSEMBLE), F32),
+        in_specs=[vmem],
+        out_specs=vmem,
+        scratch_shapes=[pltpu.VMEM((ENSEMBLE, ENSEMBLE), F32)],
+        name="factor_and_invert",
+    )(both)
 
 
 def on_device(height_velocity_tensor, obs_values, obs_precision, obs_index):

time: 161 us -> 111 us (0.69)
  other arithmetic: 55.3 us -> 0.67 us
  Pallas kernels: 94.3 us -> 108 us
  local copies, waits for them, and re-layouts: 8.1 us -> 2.46 us
  matrix products: 1.85 us -> 0 us
    another operation x9 -> x0, other arithmetic: 53.8 us -> none  [the longest x6 34.1 us: make_transform(): factor = lax.linalg.cholesky(identity + gram, symmetrize_input=False)]
    pallas_call x0 -> x1, Pallas kernels: none -> 13.5 us  [make_transform(): pl.pallas_call(transform_kernel, out_shape=jax.ShapeDtypeStruct((ENSEMBLE...]
    another operation x9 -> x0, local copies, waits for them, and re-layouts: 3.96 us -> none
    squeeze x2 -> x0, local copies, waits for them, and re-layouts: 1.68 us -> none  [the longest x1 0.92 us: make_transform(): lower = jnp.concatenate([both[0, COLS:], both[1, COLS:]], axis=1)]
where the time goes in v2:
time: 111 us
  Pallas kernels  108 us (97%)
  local copies, waits for them, and re-layouts  2.46 us (2%)
    pallas_call x1, Pallas kernels, gather(): pl.pallas_call(gather_kernel, out_shape=(jax.ShapeDtypeStruct((OWNERS, LO...  69 us
    pallas_call x1, Pallas kernels, give_back(): pl.pallas_call(return_kernel, out_shape=jax.ShapeDtypeStruct((LOCAL * FIE...  25.5 us
    pallas_call x1, Pallas kernels, make_transform(): pl.pallas_call(transform_kernel, out_shape=jax.ShapeDtypeStruct((ENSEMBLE...  13.5 us
    unnamed x5, local copies, waits for them, and re-layouts  2.38 us

profile of v2, /device:TPU:1, one launch (start us, length us, event | category | flops | bytes accessed | tf_op | source)
XLA Modules:
  0.0 111.1 jit_solution(9201852773536605968)
XLA Ops:
  0.0 0.0 copy-start.1
  0.0 0.0 copy-start
  0.0 0.1 pad.2.clone
  0.1 0.6 copy-done.1
  0.7 0.0 copy-done
  0.7 0.7 maximum_maximum_fusion.obs_ref
  1.4 69.0 %gather_and_gram.1 = (f32[32,8,384]{2,1,0:T(8,128)}, f32[2,256,128]{2,1,0:T(8,128)}) custom-call(f32[768,128]{1,0:T(8,128)} %bitcast.3, f32[24,8,4,128]{3,2,1,0:T(4,128)} %bitcast.4, f32[8,192]{1,0:T(8,128)} %maximum_maximum_fusion.obs_ref, s32[1,192]{1,0:T(1,128)} %index_ref.1), custom_call_target="tpu_custom_call" | custom-call | tf_op jit(solution)/shard_map/gather_and_gram/pallas_call | solution.py:325
  70.4 13.5 %factor_and_invert.1.transform_ref = f32[256,256]{1,0:T(8,128)} custom-call(f32[2,256,128]{2,1,0:T(8,128)} %get-tuple-element.8.both_ref), custom_call_target="tpu_custom_call" | custom-call | tf_op jit(solution)/shard_map/factor_and_invert/pallas_call | solution.py:526
  83.9 25.5 %update_and_return.1 = f32[768,128]{1,0:T(8,128)} custom-call(f32[32,8,384]{2,1,0:T(8,128)} %get-tuple-element.7.values_ref, f32[256,256]{1,0:T(8,128)} %factor_and_invert.1.transform_ref), custom_call_target="tpu_custom_call" | custom-call | tf_op jit(solution)/shard_map/update_and_return/pallas_call | solution.py:410
  109.3 1.8 %copy.6 = f32[8,3,32,128]{3,2,1,0:T(8,128)} copy(f32[8,3,32,128]{3,2,1,0:T(8,128)} %bitcast.5) | data formatting | bytes 786432
  (1 shorter events, 0.0 us)
Async XLA Ops:
  0.0 0.7 copy-start.1
  0.0 0.7 copy-start

commit v3 on v2

--- a/solution.py
+++ b/solution.py
@@ -50,6 +50,24 @@
     return {"group": k // MEMBERS, "member": lax.rem(k, MEMBERS)}
 
 
+def hops(offset):
+    return min(offset[0], GROUPS - offset[0]) + 3 * min(offset[1], 4 - offset[1])
+
+
+OFFSETS = sorted(
+    [(a, b, c) for a in range(GROUPS) for b in range(4) for c in range(2) if a + b + c],
+    key=hops,
+    reverse=True,
+)
+
+
+def other_owners(group, member):
+    z_part, core = member // 2, lax.rem(member, 2)
+    for a, b, c in OFFSETS:
+        there = lax.rem(group + a, GROUPS) * MEMBERS
+        yield there + lax.rem(z_part + b, 4) * 2 + lax.rem(core + c, 2)
+
+
 def z_id(z, core, y):
     return {"member": z // 3 * 2 + core, "space": lax.rem(z, 3) * NY_CHIPS + y}
 
@@ -88,12 +106,14 @@
 
 
 def gather_kernel(
-    x_ref,
+    x_hbm_ref,
     x_halo_ref,
-    obs_ref,
+    value_ref,
+    precision_ref,
     index_ref,
     values_ref,
     gram_ref,
+    x_ref,
     halo,
     sendbuf,
     mine,
@@ -106,6 +126,7 @@
     z_own,
     all_y,
     all_x,
+    x_in_sem,
     halo_send,
     halo_recv,
     a2a_send,
@@ -124,10 +145,14 @@
     y = lax.rem(space, NY_CHIPS)
     me = group * MEMBERS + member
 
+    x_in = pltpu.make_async_copy(x_hbm_ref, x_ref, x_in_sem)
+    x_in.start()
+
     barrier = pltpu.get_barrier_semaphore()
     above, below = lax.rem(space + SPACES - 1, SPACES), lax.rem(space + 1, SPACES)
     peers = [{"space": above}, {"space": below}]
-    peers += [owner_id(lax.rem(me + d, OWNERS)) for d in range(1, OWNERS)]
+    owners = list(other_owners(group, member))
+    peers += [owner_id(k) for k in owners]
     y_peers = [
         {"space": space - y + lax.rem(y + d, NY_CHIPS)} for d in range(1, NY_CHIPS)
     ]
@@ -138,10 +163,48 @@
 
     cells = lax.broadcasted_iota(jnp.int32, (CELLS, OBS), 0)
     picked = jnp.where(cells == index_ref[0:1, :], 1.0, 0.0)
-    spread = dot_nt(obs_ref[...], picked)
-    weight = spread[1:2, :] * SCALE
+    spread = dot_nt(jnp.broadcast_to(precision_ref[...], (SUB, OBS)), picked)
+    weight = spread[0:1, :] * SCALE
+    spread = dot_nt(jnp.broadcast_to(value_ref[...], (SUB, OBS)), picked)
     seen_value = spread[0:1, :]
 
+    flat = [halo.at[i].reshape(LOCAL * FIELDS * HALO, COLS) for i in range(2)]
+
+    def load(field, row):
+        if row < 0:
+            start = field * HALO + row + HALO
+            return flat[0][pl.ds(start, LOCAL, stride=FIELDS * HALO), :]
+        if row >= ROWS:
+            start = field * HALO + row - ROWS
+            return flat[1][pl.ds(start, LOCAL, stride=FIELDS * HALO), :]
+        return x_ref[pl.ds(field * ROWS + row, LOCAL, stride=FIELDS * ROWS), :]
+
+    first, last = space == 0, space == SPACES - 1
+
+    def outside(row):
+        return first if row < 0 else last if row >= ROWS else None
+
+    forecast = Forecast(load, outside)
+
+    def block_copy(k):
+        return pltpu.make_async_remote_copy(
+            src_ref=sendbuf.at[k],
+            dst_ref=values_ref.at[me],
+            send_sem=a2a_send.at[k],
+            recv_sem=a2a_recv.at[me],
+            device_id=owner_id(k),
+            device_id_type=MESH,
+        )
+
+    def emit(rows):
+        for row in rows:
+            for field in range(FIELDS):
+                sendbuf[row, :, field * COLS : (field + 1) * COLS] = forecast.get(
+                    field, STEPS, row
+                )
+
+    x_in.wait()
+    emit(range(HALO, ROWS - HALO))
     pl.semaphore_wait(barrier, len(peers))
 
     up = pltpu.make_async_remote_copy(
@@ -163,60 +226,28 @@
     up.start()
     down.start()
 
-    flat = [halo.at[i].reshape(LOCAL * FIELDS * HALO, COLS) for i in range(2)]
-
-    def load(field, row):
-        if row < 0:
-            start = field * HALO + row + HALO
-            return flat[0][pl.ds(start, LOCAL, stride=FIELDS * HALO), :]
-        if row >= ROWS:
-            start = field * HALO + row - ROWS
-            return flat[1][pl.ds(start, LOCAL, stride=FIELDS * HALO), :]
-        return x_ref[pl.ds(field * ROWS + row, LOCAL, stride=FIELDS * ROWS), :]
-
-    first, last = space == 0, space == SPACES - 1
-
-    def outside(row):
-        return first if row < 0 else last if row >= ROWS else None
-
-    forecast = Forecast(load, outside)
-
-    def block_copy(k):
-        return pltpu.make_async_remote_copy(
-            src_ref=sendbuf.at[k],
-            dst_ref=values_ref.at[me],
-            send_sem=a2a_send.at[k],
-            recv_sem=a2a_recv.at[me],
-            device_id=owner_id(k),
-            device_id_type=MESH,
-        )
-
-    def emit(rows):
-        for row in rows:
-            for field in range(FIELDS):
-                sendbuf[row, :, field * COLS : (field + 1) * COLS] = forecast.get(
-                    field, STEPS, row
-                )
-
-    def start(k):
-        @pl.when(k != me)
+    def is_inner(k):
+        return jnp.logical_and(k >= HALO, k < ROWS - HALO)
+
+    for k in owners:
+
+        @pl.when(is_inner(k))
         def _():
             block_copy(k).start()
 
-    inner = ROWS - 2 * HALO
-    emit(range(HALO, ROWS - HALO))
-    for d in range(inner):
-        start(HALO + lax.rem(me + d, inner))
     up.wait()
     down.wait()
     emit(list(range(HALO)) + list(range(ROWS - HALO, ROWS)))
-    for d in range(2 * HALO):
-        start(lax.rem(ROWS - HALO + lax.rem(me + d, 2 * HALO), ROWS))
+    for k in owners:
+
+        @pl.when(jnp.logical_not(is_inner(k)))
+        def _():
+            block_copy(k).start()
+
     values_ref[me] = sendbuf[me]
-    for d in range(1, OWNERS):
-        block_copy(lax.rem(me + d, OWNERS)).wait_send()
-    for d in range(1, OWNERS):
-        k = lax.rem(me + d, OWNERS)
+    for k in owners:
+        block_copy(k).wait_send()
+    for k in owners:
         pltpu.make_async_remote_copy(
             src_ref=sendbuf.at[k],
             dst_ref=values_ref.at[k],
@@ -318,8 +349,9 @@
 STEPS = 2
 
 
-def gather(state, obs, index):
+def gather(state, values, precision, index):
     vmem = pl.BlockSpec(memory_space=pltpu.VMEM)
+    hbm = pl.BlockSpec(memory_space=pltpu.HBM)
     dma = pltpu.SemaphoreType.DMA
     quarter = ENSEMBLE // GROUPS
     return pl.pallas_call(
@@ -328,9 +360,10 @@
             jax.ShapeDtypeStruct((OWNERS, LOCAL, CELLS), F32),
             jax.ShapeDtypeStruct((2, ENSEMBLE, COLS), F32),
         ),
-        in_specs=[vmem, pl.BlockSpec(memory_space=pl.ANY), vmem, vmem],
+        in_specs=[hbm, hbm, vmem, vmem, vmem],
         out_specs=(vmem, vmem),
         scratch_shapes=[
+            pltpu.VMEM((LOCAL * FIELDS * ROWS, COLS), F32),
             pltpu.VMEM((2, LOCAL * FIELDS, HALO, COLS), F32),
             pltpu.VMEM((OWNERS, LOCAL, CELLS), F32),
             pltpu.VMEM((2, ENSEMBLE, COLS), F32),
@@ -343,6 +376,7 @@
             pltpu.VMEM((8, COLS), F32),
             pltpu.VMEM((NY_CHIPS, 8, COLS), F32),
             pltpu.VMEM((GROUPS, quarter, COLS), F32),
+            dma,
             dma((2,)),
             dma((2,)),
             dma((OWNERS,)),
@@ -360,68 +394,10 @@
     )(
         state.reshape(LOCAL * FIELDS * ROWS, COLS),
         state.reshape(LOCAL * FIELDS, ROWS // HALO, HALO, COLS),
-        obs,
+        values,
+        precision,
         index,
     )
-
-
-def return_kernel(values_ref, transform_ref, out_ref, sendbuf, arrived, send_sem, recv_sem):
-    group, member, _ = place()
-    me = group * MEMBERS + member
-    barrier = pltpu.get_barrier_semaphore()
-    for d in range(1, OWNERS):
-        pl.semaphore_signal(
-            barrier, inc=1, device_id=owner_id(lax.rem(me + d, OWNERS)), device_id_type=MESH
-        )
-    values = values_ref[...].reshape(ENSEMBLE, CELLS)
-    mean = jnp.sum(values, axis=0, keepdims=True) * (1.0 / ENSEMBLE)
-    updated = dot_nn(transform_ref[...], values - mean) + mean
-    sendbuf[...] = updated.reshape(OWNERS, LOCAL, CELLS)
-    pl.semaphore_wait(barrier, OWNERS - 1)
-
-    def copy(k, slot):
-        return pltpu.make_async_remote_copy(
-            src_ref=sendbuf.at[k],
-            dst_ref=arrived.at[slot],
-            send_sem=send_sem.at[k],
-            recv_sem=recv_sem.at[slot],
-            device_id=owner_id(k),
-            device_id_type=MESH,
-        )
-
-    for d in range(1, OWNERS):
-        copy(lax.rem(me + d, OWNERS), me).start()
-    arrived[me] = sendbuf[me]
-    for d in range(1, OWNERS):
-        copy(lax.rem(me + d, OWNERS), me).wait_send()
-    for d in range(1, OWNERS):
-        k = lax.rem(me + d, OWNERS)
-        copy(k, k).wait_recv()
-    for row in range(ROWS):
-        for field in range(FIELDS):
-            out_ref[pl.ds(field * ROWS + row, LOCAL, stride=FIELDS * ROWS), :] = arrived[
-                row, :, field * COLS : (field + 1) * COLS
-            ]
-
-
-def give_back(values, transform):
-    vmem = pl.BlockSpec(memory_space=pltpu.VMEM)
-    dma = pltpu.SemaphoreType.DMA
-    out = pl.pallas_call(
-        return_kernel,
-        out_shape=jax.ShapeDtypeStruct((LOCAL * FIELDS * ROWS, COLS), F32),
-        in_specs=[vmem, vmem],
-        out_specs=vmem,
-        scratch_shapes=[
-            pltpu.VMEM((OWNERS, LOCAL, CELLS), F32),
-            pltpu.VMEM((OWNERS, LOCAL, CELLS), F32),
-            dma((OWNERS,)),
-            dma((OWNERS,)),
-        ],
-        compiler_params=pltpu.CompilerParams(collective_id=1, has_side_effects=True),
-        name="update_and_return",
-    )(values, transform)
-    return out.reshape(LOCAL, FIELDS, ROWS, COLS)
 
 
 def lane(tile, at):
@@ -502,7 +478,7 @@
             work[rest, own] = jnp.zeros((ENSEMBLE - at - BLOCK, BLOCK), F32)
             work[rest, :] = work[rest, :] - dot_nn(factor, solved)
 
-def transform_kernel(both_ref, transform_ref, work):
+def make_transform(both_ref, work):
     r = lax.broadcasted_iota(jnp.int32, (COLS, COLS), 0)
     c = lax.broadcasted_iota(jnp.int32, (COLS, COLS), 1)
     eye = jnp.where(r == c, 1.0, 0.0)
@@ -518,25 +494,71 @@
     inverse = jnp.where(r >= c, work[...], 0.0)
     inner = dot_nt(jnp.broadcast_to(pull, (SUB, ENSEMBLE)), inverse)
     weights = dot_nn(inner, inverse)
-    transform_ref[...] = inverse + weights[0:1, :]
-
-
-def make_transform(both):
+    return inverse + weights[0:1, :]
+
+
+def return_kernel(values_ref, both_ref, out_ref, work, sendbuf, arrived, send_sem, recv_sem):
+    group, member, _ = place()
+    me = group * MEMBERS + member
+    barrier = pltpu.get_barrier_semaphore()
+    owners = list(other_owners(group, member))
+    for k in owners:
+        pl.semaphore_signal(barrier, inc=1, device_id=owner_id(k), device_id_type=MESH)
+    transform = make_transform(both_ref, work)
+    values = values_ref[...].reshape(ENSEMBLE, CELLS)
+    mean = jnp.sum(values, axis=0, keepdims=True) * (1.0 / ENSEMBLE)
+    updated = dot_nn(transform, values - mean) + mean
+    sendbuf[...] = updated.reshape(OWNERS, LOCAL, CELLS)
+    pl.semaphore_wait(barrier, OWNERS - 1)
+
+    def copy(k, slot):
+        return pltpu.make_async_remote_copy(
+            src_ref=sendbuf.at[k],
+            dst_ref=arrived.at[slot],
+            send_sem=send_sem.at[k],
+            recv_sem=recv_sem.at[slot],
+            device_id=owner_id(k),
+            device_id_type=MESH,
+        )
+
+    for k in owners:
+        copy(k, me).start()
+    arrived[me] = sendbuf[me]
+    for k in owners:
+        copy(k, me).wait_send()
+    for k in owners:
+        copy(k, k).wait_recv()
+    for row in range(ROWS):
+        for field in range(FIELDS):
+            out_ref[pl.ds(field * ROWS + row, LOCAL, stride=FIELDS * ROWS), :] = arrived[
+                row, :, field * COLS : (field + 1) * COLS
+            ]
+
+
+def give_back(values, both):
     vmem = pl.BlockSpec(memory_space=pltpu.VMEM)
-    return pl.pallas_call(
-        transform_kernel,
-        out_shape=jax.ShapeDtypeStruct((ENSEMBLE, ENSEMBLE), F32),
-        in_specs=[vmem],
+    dma = pltpu.SemaphoreType.DMA
+    out = pl.pallas_call(
+        return_kernel,
+        out_shape=jax.ShapeDtypeStruct((LOCAL * FIELDS * ROWS, COLS), F32),
+        in_specs=[vmem, vmem],
         out_specs=vmem,
-        scratch_shapes=[pltpu.VMEM((ENSEMBLE, ENSEMBLE), F32)],
-        name="factor_and_invert",
-    )(both)
+        scratch_shapes=[
+            pltpu.VMEM((ENSEMBLE, ENSEMBLE), F32),
+            pltpu.VMEM((OWNERS, LOCAL, CELLS), F32),
+            pltpu.VMEM((OWNERS, LOCAL, CELLS), F32),
+            dma((OWNERS,)),
+            dma((OWNERS,)),
+        ],
+        compiler_params=pltpu.CompilerParams(collective_id=1, has_side_effects=True),
+        name="transform_and_return",
+    )(values, both)
+    return out.reshape(LOCAL, FIELDS, ROWS, COLS)
 
 
 def on_device(height_velocity_tensor, obs_values, obs_precision, obs_index):
-    obs = jnp.concatenate([obs_values, obs_precision, jnp.zeros((6, OBS), F32)], axis=0)
-    values, both = gather(height_velocity_tensor, obs, obs_index)
-    return give_back(values, make_transform(both))
+    values, both = gather(height_velocity_tensor, obs_values, obs_precision, obs_index)
+    return give_back(values, both)
 
 
 def solution(mesh):

time: 111 us -> 101 us (0.910)
  Pallas kernels: 108 us -> 99.3 us
    pallas_call x1 -> x0, Pallas kernels: 13.5 us -> none  [make_transform(): pl.pallas_call(transform_kernel, out_shape=jax.ShapeDtypeStruct((ENSEMBLE...]
    pallas_call x1, Pallas kernels: 25.5 us -> 30.8 us  [give_back(): pl.pallas_call(return_kernel, out_shape=jax.ShapeDtypeStruct((LOCAL * FIE...]
    unnamed x5 -> x1, local copies, waits for them, and re-layouts: 2.38 us -> 1.77 us
where the time goes in v3:
time: 101 us
  Pallas kernels  99.3 us (98%)
  local copies, waits for them, and re-layouts  1.77 us (2%)
    pallas_call x1, Pallas kernels, gather(): pl.pallas_call(gather_kernel, out_shape=(jax.ShapeDtypeStruct((OWNERS, LO...  68.5 us
    pallas_call x1, Pallas kernels, give_back(): pl.pallas_call(return_kernel, out_shape=jax.ShapeDtypeStruct((LOCAL * FIE...  30.8 us

profile of v3, /device:TPU:1, one launch (start us, length us, event | category | flops | bytes accessed | tf_op | source)
XLA Modules:
  0.0 101.1 jit_solution(1081558301211514476)
XLA Ops:
  0.0 68.5 %gather_and_gram.1 = (f32[32,8,384]{2,1,0:T(8,128)}, f32[2,256,128]{2,1,0:T(8,128)}) custom-call(f32[768,128]{1,0:T(8,128)} %bitcast.3, f32[24,8,4,128]{3,2,1,0:T(4,128)} %bitcast.4, f32[1,192]{1,0:T(1,128)} %value_ref.1, f32[1,192]{1,0:T(1,128)} %precision_ref.1, s32[1,192]{1,0:T(1,128)} %index_ref.1), custom_call_target="tpu_custom_call" | custom-call | tf_op jit(solution)/shard_map/gather_and_gram/pallas_call | solution.py:357
  68.5 30.8 %transform_and_return.1 = f32[768,128]{1,0:T(8,128)} custom-call(f32[32,8,384]{2,1,0:T(8,128)} %get-tuple-element.7.values_ref, f32[2,256,128]{2,1,0:T(8,128)} %get-tuple-element.8.both_ref), custom_call_target="tpu_custom_call" | custom-call | tf_op jit(solution)/shard_map/transform_and_return/pallas_call | solution.py:541
  99.3 1.8 %copy.6 = f32[8,3,32,128]{3,2,1,0:T(8,128)} copy(f32[8,3,32,128]{3,2,1,0:T(8,128)} %bitcast.5) | data formatting | bytes 786432

commit v4 on v3

--- a/solution.py
+++ b/solution.py
@@ -48,6 +48,9 @@
 
 def owner_id(k):
     return {"group": k // MEMBERS, "member": lax.rem(k, MEMBERS)}
+
+
+SETS = [(2, 0), (2, 1), (1, 0), (1, 1), (3, 0), (3, 1), (0, 1)]
 
 
 def hops(offset):
@@ -124,8 +127,6 @@
     y_to,
     z_from,
     z_own,
-    all_y,
-    all_x,
     x_in_sem,
     halo_send,
     halo_recv,
@@ -137,7 +138,6 @@
     z_sem,
     gy_sem,
     gx_sem,
-    gc_sem,
 ):
     group, member, space = place()
     core = lax.rem(member, 2)
@@ -321,29 +321,21 @@
     for at in range(1, NZ):
         total = total + z_from[at]
 
-    all_y[y] = total
+    own = gram_ref.at[core, group]
+    own[y] = total
     copies = []
     for d in range(1, NY_CHIPS):
-        copies.append(
-            exchange(all_y.at[y], all_y.at[y], gy_sem, d - 1, d - 1, y_peers[d - 1])
-        )
+        copies.append(exchange(own.at[y], own.at[y], gy_sem, d - 1, d - 1, y_peers[d - 1]))
     for copy in copies:
         copy.wait()
 
-    x_slice = all_y[...].reshape(ENSEMBLE // GROUPS, COLS)
-    all_x[group] = x_slice
     copies = []
-    for d in range(1, GROUPS):
-        there = lax.rem(group + d, GROUPS)
-        copies.append(
-            exchange(all_x.at[group], all_x.at[group], gx_sem, d - 1, d - 1, {"group": there})
-        )
+    for slot, (step, other) in enumerate(SETS):
+        there = lax.rem(group + step, GROUPS)
+        device = {"group": there, "member": member + other * (1 - 2 * core)}
+        copies.append(exchange(own, own, gx_sem, slot, slot, device))
     for copy in copies:
         copy.wait()
-
-    gram_ref[core] = all_x[...].reshape(ENSEMBLE, COLS)
-    copy = exchange(gram_ref.at[core], gram_ref.at[core], gc_sem, 0, 0, partner)
-    copy.wait()
 
 
 STEPS = 2
@@ -358,7 +350,7 @@
         gather_kernel,
         out_shape=(
             jax.ShapeDtypeStruct((OWNERS, LOCAL, CELLS), F32),
-            jax.ShapeDtypeStruct((2, ENSEMBLE, COLS), F32),
+            jax.ShapeDtypeStruct((2, GROUPS, NY_CHIPS, 8, COLS), F32),
         ),
         in_specs=[hbm, hbm, vmem, vmem, vmem],
         out_specs=(vmem, vmem),
@@ -374,8 +366,6 @@
             pltpu.VMEM((NY_CHIPS, 8, COLS), F32),
             pltpu.VMEM((NZ, 8, COLS), F32),
             pltpu.VMEM((8, COLS), F32),
-            pltpu.VMEM((NY_CHIPS, 8, COLS), F32),
-            pltpu.VMEM((GROUPS, quarter, COLS), F32),
             dma,
             dma((2,)),
             dma((2,)),
@@ -386,8 +376,7 @@
             dma((2, NY_CHIPS - 1)),
             dma((2, NZ - 1)),
             dma((2, NY_CHIPS - 1)),
-            dma((2, GROUPS - 1)),
-            dma((2, 1)),
+            dma((2, len(SETS))),
         ],
         compiler_params=pltpu.CompilerParams(collective_id=0, has_side_effects=True),
         name="gather_and_gram",
@@ -417,14 +406,20 @@
     columns = [lane(tile, at + j) for j in range(SUB)]
     left = {(i, j): sublane(columns[j], i) for j in range(SUB) for i in range(j, SUB)}
     low, inv = {}, {}
-    for j in range(SUB):
-        root = lax.rsqrt(left[j, j])
+    for j in range(0, SUB, 2):
+        n = j + 1
+        first, cross, second = left[j, j], left[n, j], left[n, n]
+        root = lax.rsqrt(first)
+        root_pair = lax.rsqrt(first * second - cross * cross)
         inv[j, j] = root
-        for i in range(j + 1, SUB):
+        inv[n, n] = root_pair * (first * root)
+        for i in range(n, SUB):
             low[i, j] = left[i, j] * root
-        for k in range(j + 1, SUB):
+        for i in range(n + 1, SUB):
+            low[i, n] = (left[i, n] - low[i, j] * low[n, j]) * inv[n, n]
+        for k in range(n + 1, SUB):
             for i in range(k, SUB):
-                left[i, k] = left[i, k] - low[i, j] * low[k, j]
+                left[i, k] = left[i, k] - low[i, j] * low[k, j] - low[i, n] * low[k, n]
     for j in range(SUB):
         for i in range(j + 1, SUB):
             terms = [low[i, k] * inv[k, j] for k in range(j, i)]
@@ -482,12 +477,13 @@
     r = lax.broadcasted_iota(jnp.int32, (COLS, COLS), 0)
     c = lax.broadcasted_iota(jnp.int32, (COLS, COLS), 1)
     eye = jnp.where(r == c, 1.0, 0.0)
-    below = both_ref[0, COLS:, :]
-    work[:COLS, :COLS] = both_ref[0, :COLS, :] + eye
-    work[COLS:, :COLS] = below
-    work[:COLS, COLS:] = below.T
-    work[COLS:, COLS:] = both_ref[1, COLS:, :] + eye
-    pull = jnp.concatenate([both_ref[1, 0:1, :], both_ref[1, 1:2, :]], axis=1)
+    left = both_ref[0].reshape(ENSEMBLE, COLS)
+    right = both_ref[1].reshape(ENSEMBLE, COLS)
+    work[:COLS, :COLS] = left[:COLS] + eye
+    work[COLS:, :COLS] = left[COLS:]
+    work[:COLS, COLS:] = left[COLS:].T
+    work[COLS:, COLS:] = right[COLS:] + eye
+    pull = jnp.concatenate([right[0:1], right[1:2]], axis=1)
     invert(work)
     r = lax.broadcasted_iota(jnp.int32, (ENSEMBLE, ENSEMBLE), 0)
     c = lax.broadcasted_iota(jnp.int32, (ENSEMBLE, ENSEMBLE), 1)

time: 101 us -> 99.2 us (0.982)
  Pallas kernels: 99.3 us -> 97.2 us
    pallas_call x1, Pallas kernels: 68.5 us -> 67.1 us  [gather(): pl.pallas_call(gather_kernel, out_shape=(jax.ShapeDtypeStruct((OWNERS, LO...]
where the time goes in v4:
time: 99.2 us; the launch traced here: 99 us
  Pallas kernels  97.2 us (98%)
  local copies, waits for them, and re-layouts  1.77 us (2%)
    pallas_call x1, Pallas kernels, gather(): pl.pallas_call(gather_kernel, out_shape=(jax.ShapeDtypeStruct((OWNERS, LO...  67.1 us
    pallas_call x1, Pallas kernels, give_back(): pl.pallas_call(return_kernel, out_shape=jax.ShapeDtypeStruct((LOCAL * FIE...  30.2 us

profile of v4, /device:TPU:1, one launch (start us, length us, event | category | flops | bytes accessed | tf_op | source)
XLA Modules:
  0.0 99.0 jit_solution(16718003793337051360)
XLA Ops:
  0.0 67.1 %gather_and_gram.1 = (f32[32,8,384]{2,1,0:T(8,128)}, f32[2,4,8,8,128]{4,3,2,1,0:T(8,128)}) custom-call(f32[768,128]{1,0:T(8,128)} %bitcast.3, f32[24,8,4,128]{3,2,1,0:T(4,128)} %bitcast.4, f32[1,192]{1,0:T(1,128)} %value_ref.1, f32[1,192]{1,0:T(1,128)} %precision_ref.1, s32[1,192]{1,0:T(1,128)} %index_ref.1), custom_call_target="tpu_custom_call" | custom-call | tf_op jit(solution)/shard_map/gather_and_gram/pallas_call | solution.py:349
  67.1 30.2 %transform_and_return.1 = f32[768,128]{1,0:T(8,128)} custom-call(f32[32,8,384]{2,1,0:T(8,128)} %get-tuple-element.7.values_ref, f32[2,4,8,8,128]{4,3,2,1,0:T(8,128)} %get-tuple-element.8.both_ref), custom_call_target="tpu_custom_call" | custom-call | tf_op jit(solution)/shard_map/transform_and_return/pallas_call | solution.py:537
  97.2 1.8 %copy.6 = f32[8,3,32,128]{3,2,1,0:T(8,128)} copy(f32[8,3,32,128]{3,2,1,0:T(8,128)} %bitcast.5) | data formatting | bytes 786432

commit v5 on v4

--- a/solution.py
+++ b/solution.py
@@ -402,8 +402,7 @@
         )
     return terms[0]
 
-def small_factor(tile, at):
-    columns = [lane(tile, at + j) for j in range(SUB)]
+def small_factor(columns):
     left = {(i, j): sublane(columns[j], i) for j in range(SUB) for i in range(j, SUB)}
     low, inv = {}, {}
     for j in range(0, SUB, 2):
@@ -431,8 +430,9 @@
     tiles = [wide[SUB * q : SUB * (q + 1)] for q in range(BLOCK // SUB)]
     rows = lax.broadcasted_iota(jnp.int32, (SUB, COLS), 0)
     count = len(tiles)
+    columns = [lane(tiles[0], j) for j in range(SUB)]
     for p in range(count):
-        inv = small_factor(tiles[p], SUB * p)
+        inv = small_factor(columns)
         terms = []
         for j in range(SUB):
             column = inv[SUB - 1, j]
@@ -445,11 +445,14 @@
         spread = [sublane(done, k) for k in range(SUB)]
         for q in range(p + 1, count):
             source = [lane(tiles[q], SUB * p + j) for j in range(SUB)]
-            terms = [
-                total([inv[k, j] * source[j] for j in range(k + 1)]) * spread[k]
-                for k in range(SUB)
-            ]
-            tiles[q] = tiles[q] - total(terms)
+            low = [total([inv[k, j] * source[j] for j in range(k + 1)]) for k in range(SUB)]
+            if q == p + 1:
+                columns = [
+                    lane(tiles[q], SUB * q + j)
+                    - total([low[k] * sublane(low[k], j) for k in range(SUB)])
+                    for j in range(SUB)
+                ]
+            tiles[q] = tiles[q] - total([low[k] * spread[k] for k in range(SUB)])
         tiles[p] = done
     return jnp.concatenate(tiles, axis=0)[:, BLOCK:]
 

time: 99.2 us -> 96 us (0.968)
  Pallas kernels: 97.2 us -> 93.9 us
    pallas_call x1, Pallas kernels: 30.2 us -> 26.9 us  [give_back(): pl.pallas_call(return_kernel, out_shape=jax.ShapeDtypeStruct((LOCAL * FIE...]
where the time goes in v5:
time: 96 us; the launch traced here: 95.7 us
  Pallas kernels  93.9 us (98%)
  local copies, waits for them, and re-layouts  1.77 us (2%)
    pallas_call x1, Pallas kernels, gather(): pl.pallas_call(gather_kernel, out_shape=(jax.ShapeDtypeStruct((OWNERS, LO...  67.1 us
    pallas_call x1, Pallas kernels, give_back(): pl.pallas_call(return_kernel, out_shape=jax.ShapeDtypeStruct((LOCAL * FIE...  26.9 us

profile of v5, /device:TPU:1, one launch (start us, length us, event | category | flops | bytes accessed | tf_op | source)
XLA Modules:
  0.0 95.7 jit_solution(12233598598701764396)
XLA Ops:
  0.0 67.1 %gather_and_gram.1 = (f32[32,8,384]{2,1,0:T(8,128)}, f32[2,4,8,8,128]{4,3,2,1,0:T(8,128)}) custom-call(f32[768,128]{1,0:T(8,128)} %bitcast.3, f32[24,8,4,128]{3,2,1,0:T(4,128)} %bitcast.4, f32[1,192]{1,0:T(1,128)} %value_ref.1, f32[1,192]{1,0:T(1,128)} %precision_ref.1, s32[1,192]{1,0:T(1,128)} %index_ref.1), custom_call_target="tpu_custom_call" | custom-call | tf_op jit(solution)/shard_map/gather_and_gram/pallas_call | solution.py:349
  67.1 26.9 %transform_and_return.1 = f32[768,128]{1,0:T(8,128)} custom-call(f32[32,8,384]{2,1,0:T(8,128)} %get-tuple-element.7.values_ref, f32[2,4,8,8,128]{4,3,2,1,0:T(8,128)} %get-tuple-element.8.both_ref), custom_call_target="tpu_custom_call" | custom-call | tf_op jit(solution)/shard_map/transform_and_return/pallas_call | solution.py:540
  94.0 1.8 %copy.6 = f32[8,3,32,128]{3,2,1,0:T(8,128)} copy(f32[8,3,32,128]{3,2,1,0:T(8,128)} %bitcast.5) | data formatting | bytes 786432

commit v6 on v5

--- a/solution.py
+++ b/solution.py
@@ -285,25 +285,30 @@
     copy = exchange(mine.at[1 - core], corebuf, core_sem, 0, 0, partner)
     copy.wait()
     half = mine[core] + corebuf[...]
-    x_to[...] = half.reshape(GROUPS, ENSEMBLE // GROUPS, COLS)
-
+    x_to[...] = half.reshape(GROUPS, NY_CHIPS, 8, COLS)
+
+    order = (4, 3, 5, 2, 6, 1, 7, 0)
+    x_copies = {}
+    for e in order:
+        piece = lax.rem(y + e, NY_CHIPS)
+        for d in range(1, GROUPS):
+            there = lax.rem(group + d, GROUPS)
+            sem_at = (d - 1) * NY_CHIPS + e
+            src, dst = x_to.at[there, piece], x_from.at[d - 1, piece]
+            x_copies[e, d] = exchange(src, dst, x_sem, sem_at, sem_at, {"group": there})
     copies = []
-    for d in range(1, GROUPS):
-        there = lax.rem(group + d, GROUPS)
-        copies.append(
-            exchange(x_to.at[there], x_from.at[d - 1], x_sem, d - 1, d - 1, {"group": there})
+    for e in order:
+        piece = lax.rem(y + e, NY_CHIPS)
+        for d in range(1, GROUPS):
+            x_copies[e, d].wait_recv()
+        y_to[piece] = x_to[group, piece] + (
+            x_from[0, piece] + x_from[1, piece] + x_from[2, piece]
         )
-    for copy in copies:
-        copy.wait()
-    quarter = x_to[group] + (x_from[0] + x_from[1] + x_from[2])
-    y_to[...] = quarter.reshape(NY_CHIPS, 8, COLS)
-
-    copies = []
-    for d in range(1, NY_CHIPS):
-        there = lax.rem(y + d, NY_CHIPS)
-        copies.append(
-            exchange(y_to.at[there], y_from.at[d - 1], y_sem, d - 1, d - 1, y_peers[d - 1])
-        )
+        if e > 0:
+            src, dst = y_to.at[piece], y_from.at[e - 1]
+            copies.append(exchange(src, dst, y_sem, e - 1, e - 1, y_peers[e - 1]))
+    for copy in x_copies.values():
+        copy.wait_send()
     for copy in copies:
         copy.wait()
     tile = y_to[y]
@@ -345,7 +350,6 @@
     vmem = pl.BlockSpec(memory_space=pltpu.VMEM)
     hbm = pl.BlockSpec(memory_space=pltpu.HBM)
     dma = pltpu.SemaphoreType.DMA
-    quarter = ENSEMBLE // GROUPS
     return pl.pallas_call(
         gather_kernel,
         out_shape=(
@@ -360,8 +364,8 @@
             pltpu.VMEM((OWNERS, LOCAL, CELLS), F32),
             pltpu.VMEM((2, ENSEMBLE, COLS), F32),
             pltpu.VMEM((ENSEMBLE, COLS), F32),
-            pltpu.VMEM((GROUPS - 1, quarter, COLS), F32),
-            pltpu.VMEM((GROUPS, quarter, COLS), F32),
+            pltpu.VMEM((GROUPS - 1, NY_CHIPS, 8, COLS), F32),
+            pltpu.VMEM((GROUPS, NY_CHIPS, 8, COLS), F32),
             pltpu.VMEM((NY_CHIPS - 1, 8, COLS), F32),
             pltpu.VMEM((NY_CHIPS, 8, COLS), F32),
             pltpu.VMEM((NZ, 8, COLS), F32),
@@ -372,7 +376,7 @@
             dma((OWNERS,)),
             dma((OWNERS,)),
             dma((2, 1)),
-            dma((2, GROUPS - 1)),
+            dma((2, (GROUPS - 1) * NY_CHIPS)),
             dma((2, NY_CHIPS - 1)),
             dma((2, NZ - 1)),
             dma((2, NY_CHIPS - 1)),
@@ -504,10 +508,10 @@
     for k in owners:
         pl.semaphore_signal(barrier, inc=1, device_id=owner_id(k), device_id_type=MESH)
     transform = make_transform(both_ref, work)
+    work[...] = transform
     values = values_ref[...].reshape(ENSEMBLE, CELLS)
     mean = jnp.sum(values, axis=0, keepdims=True) * (1.0 / ENSEMBLE)
-    updated = dot_nn(transform, values - mean) + mean
-    sendbuf[...] = updated.reshape(OWNERS, LOCAL, CELLS)
+    anomaly = values - mean
     pl.semaphore_wait(barrier, OWNERS - 1)
 
     def copy(k, slot):
@@ -520,8 +524,16 @@
             device_id_type=MESH,
         )
 
-    for k in owners:
-        copy(k, me).start()
+    share = ENSEMBLE // GROUPS
+    for step in (2, 1, 3, 0):
+        there = lax.rem(group + step, GROUPS)
+        part = dot_nn(work[pl.ds(pl.multiple_of(there * share, share), share), :], anomaly)
+        sendbuf[pl.ds(there * MEMBERS, MEMBERS)] = (part + mean).reshape(
+            MEMBERS, LOCAL, CELLS
+        )
+        for k, offset in zip(owners, OFFSETS):
+            if offset[0] == step:
+                copy(k, me).start()
     arrived[me] = sendbuf[me]
     for k in owners:
         copy(k, me).wait_send()

time: 96 us -> 95.7 us (level)
  no operation moved by 1% of the time
where the time goes in v6:
time: 95.7 us; the launch traced here: 95.2 us
  Pallas kernels  93.5 us (98%)
  local copies, waits for them, and re-layouts  1.77 us (2%)
    pallas_call x1, Pallas kernels, gather(): pl.pallas_call(gather_kernel, out_shape=(jax.ShapeDtypeStruct((OWNERS, LO...  66.6 us
    pallas_call x1, Pallas kernels, give_back(): pl.pallas_call(return_kernel, out_shape=jax.ShapeDtypeStruct((LOCAL * FIE...  26.8 us

profile of v6, /device:TPU:1, one launch (start us, length us, event | category | flops | bytes accessed | tf_op | source)
XLA Modules:
  0.0 95.2 jit_solution(7166697424579638579)
XLA Ops:
  0.0 66.6 %gather_and_gram.1 = (f32[32,8,384]{2,1,0:T(8,128)}, f32[2,4,8,8,128]{4,3,2,1,0:T(8,128)}) custom-call(f32[768,128]{1,0:T(8,128)} %bitcast.3, f32[24,8,4,128]{3,2,1,0:T(4,128)} %bitcast.4, f32[1,192]{1,0:T(1,128)} %value_ref.1, f32[1,192]{1,0:T(1,128)} %precision_ref.1, s32[1,192]{1,0:T(1,128)} %index_ref.1), custom_call_target="tpu_custom_call" | custom-call | tf_op jit(solution)/shard_map/gather_and_gram/pallas_call | solution.py:353
  66.6 26.8 %transform_and_return.1 = f32[768,128]{1,0:T(8,128)} custom-call(f32[32,8,384]{2,1,0:T(8,128)} %get-tuple-element.7.values_ref, f32[2,4,8,8,128]{4,3,2,1,0:T(8,128)} %get-tuple-element.8.both_ref), custom_call_target="tpu_custom_call" | custom-call | tf_op jit(solution)/shard_map/transform_and_return/pallas_call | solution.py:552
  93.5 1.8 %copy.6 = f32[8,3,32,128]{3,2,1,0:T(8,128)} copy(f32[8,3,32,128]{3,2,1,0:T(8,128)} %bitcast.5) | data formatting | bytes 786432

commit v7 on v6

--- a/solution.py
+++ b/solution.py
@@ -318,7 +318,7 @@
     z_own[...] = tile
     z_from[z] = tile
     copies = []
-    for d in range(1, NZ):
+    for d in (6, 5, 7, 4, 8, 3, 9, 2, 10, 1, 11):
         copies.append(exchange(z_own, z_from.at[z], z_sem, d - 1, d - 1, z_peers[d - 1]))
     for copy in copies:
         copy.wait()
@@ -329,7 +329,7 @@
     own = gram_ref.at[core, group]
     own[y] = total
     copies = []
-    for d in range(1, NY_CHIPS):
+    for d in (4, 3, 5, 2, 6, 1, 7):
         copies.append(exchange(own.at[y], own.at[y], gy_sem, d - 1, d - 1, y_peers[d - 1]))
     for copy in copies:
         copy.wait()
@@ -466,12 +466,16 @@
     c = lax.broadcasted_iota(jnp.int32, (BLOCK, BLOCK), 1)
     identity = jnp.where(r == c, 1.0, 0.0)
     zero = jnp.zeros((BLOCK, BLOCK), F32)
+    diagonal = work[:BLOCK, :BLOCK]
     for k in range(n):
         at = k * BLOCK
         own = slice(at, at + BLOCK)
         rest = slice(at + BLOCK, ENSEMBLE)
-        inverse = invert_block(work[own, own], identity)
+        following = slice(at + BLOCK, at + 2 * BLOCK)
+        inverse = invert_block(diagonal, identity)
         if k < n - 1:
+            near = dot_nt(work[following, own], inverse)
+            diagonal = work[following, following] - dot_nt(near, near)
             factor = dot_nt(work[rest, own], inverse)
         work[own, own] = identity
         solved = dot_nn(inverse, work[own, :])
@@ -479,6 +483,7 @@
         if k < n - 1:
             work[rest, own] = jnp.zeros((ENSEMBLE - at - BLOCK, BLOCK), F32)
             work[rest, :] = work[rest, :] - dot_nn(factor, solved)
+
 
 def make_transform(both_ref, work):
     r = lax.broadcasted_iota(jnp.int32, (COLS, COLS), 0)

time: 95.7 us -> 95.9 us (level)
  no operation moved by 1% of the time
where the time goes in v7:
time: 95.9 us; the launch traced here: 95.7 us
  Pallas kernels  93.9 us (98%)
  local copies, waits for them, and re-layouts  1.77 us (2%)
    pallas_call x1, Pallas kernels, gather(): pl.pallas_call(gather_kernel, out_shape=(jax.ShapeDtypeStruct((OWNERS, LO...  66.3 us
    pallas_call x1, Pallas kernels, give_back(): pl.pallas_call(return_kernel, out_shape=jax.ShapeDtypeStruct((LOCAL * FIE...  27.6 us

profile of v7, /device:TPU:1, one launch (start us, length us, event | category | flops | bytes accessed | tf_op | source)
XLA Modules:
  0.0 95.7 jit_solution(17228885701185518965)
XLA Ops:
  0.0 66.3 %gather_and_gram.1 = (f32[32,8,384]{2,1,0:T(8,128)}, f32[2,4,8,8,128]{4,3,2,1,0:T(8,128)}) custom-call(f32[768,128]{1,0:T(8,128)} %bitcast.3, f32[24,8,4,128]{3,2,1,0:T(4,128)} %bitcast.4, f32[1,192]{1,0:T(1,128)} %value_ref.1, f32[1,192]{1,0:T(1,128)} %precision_ref.1, s32[1,192]{1,0:T(1,128)} %index_ref.1), custom_call_target="tpu_custom_call" | custom-call | tf_op jit(solution)/shard_map/gather_and_gram/pallas_call | solution.py:353
  66.3 27.6 %transform_and_return.1 = f32[768,128]{1,0:T(8,128)} custom-call(f32[32,8,384]{2,1,0:T(8,128)} %get-tuple-element.7.values_ref, f32[2,4,8,8,128]{4,3,2,1,0:T(8,128)} %get-tuple-element.8.both_ref), custom_call_target="tpu_custom_call" | custom-call | tf_op jit(solution)/shard_map/transform_and_return/pallas_call | solution.py:557
  93.9 1.8 %copy.6 = f32[8,3,32,128]{3,2,1,0:T(8,128)} copy(f32[8,3,32,128]{3,2,1,0:T(8,128)} %bitcast.5) | data formatting | bytes 786432
